TPU v7x, 128 devices: a whole 4x4x4 slice. The times are simulated.
128 devices in a mesh: head: 8 (over x_hi, z), ctx: 16 (over y, x_lo, core).
Axes of the slice: x: 4 (x_hi: 2, x_lo: 2; x = x_hi * 2 + x_lo), y: 4, z: 4, core: 2. Of those that a mesh axis runs over, the one named last changes fastest.
Arguments:
- inputs: bfloat16 [4096, 4096], P('ctx'), may hold values from -8 to 8
- out_grad: bfloat16 [4096, 4096], P('ctx', 'head'), may hold values from -6 to 6
- w_query: bfloat16 [4096, 4096], P(None, 'head'), may hold values from -4 to 4
- w_key: bfloat16 [4096, 1024], P(None, 'head'), may hold values from -4 to 4
- value_projection: bfloat16 [4096, 1024], P(None, 'head'), may hold values from -0.09375 to 0.09375
- w_out: bfloat16 [4096, 4096], P('head'), may hold values from -0.09375 to 0.09375
- doc_lengths: int32 [8], replicated, may hold values from 1 to 2048, 4096 in all
- span_order: int32 [32], replicated, may hold values from 0 to 31, as said below
Outputs:
- input_grad: bfloat16 [4096, 4096], P('ctx', 'head')
Inputs may be any that keep to these rules, and one draw needn't show every extreme that they name: `span_order`: A permutation of 0 to 31; entries 2 d and 2 d + 1 are c and 31 - c for some c, in either order.
All inputs are finite; a program needn't handle non-finite values.
Results may differ from a plain program's by a relative error of at most 0.012.
The roundings to bfloat16 on the way count: a program that leaves them out, or rounds other values in their place, can miss the bound.
Values may be sent and summed in bfloat16 or wider, within the bound.
A program may use at most 64 MiB of HBM per device.

v0:
```python
import math

import jax
import jax.numpy as jnp
from jax import lax
from jax.sharding import Mesh
from jax.sharding import PartitionSpec as P

ASKER_NUM = 32
SHARED_KV_NUM = 8
CHANNEL_DIM = 128
HEAD = ("head_0", "head_1")


masked_score = -1e30


def in_order(parts, dim):
    lengths = list(parts.shape[1:])
    lengths[dim] *= parts.shape[0]
    return jnp.moveaxis(parts, 0, dim).reshape(lengths)


def copy_for_each(value, axis):
    copies = jnp.broadcast_to(value, (lax.axis_size(axis), *value.shape))
    return lax.all_to_all(copies, axis, split_axis=0, concat_axis=0, tiled=True)


def gathered_copies(value, axis, dim):
    return in_order(copy_for_each(value, axis), dim)


def sum_in_order(parts, axes, sequence):
    lengths = [lax.axis_size(a) for a in axes]
    parts = parts.reshape(*lengths, *parts.shape[1:])
    parts = parts.transpose(*sequence, *range(len(axes), parts.ndim))
    parts = parts.reshape(-1, *parts.shape[len(axes) :])
    for k in sequence:
        parts = lax.psum_scatter(parts, axes[k], scatter_dimension=0, tiled=True)
    return parts[0]


def split_up(value, dim, peers):
    lengths = value.shape
    parts = value.reshape(*lengths[:dim], peers, lengths[dim] // peers, *lengths[dim + 1 :])
    return jnp.moveaxis(parts, dim, 0)


def summed_rows(value, axes, sequence, dim):
    peers = lax.axis_size(axes)
    return sum_in_order(split_up(value, dim, peers), axes, sequence)


def doc_index(positions, doc_lengths):
    ends = jnp.cumsum(doc_lengths)
    return jnp.sum((positions[:, None] >= ends[None, :]).astype(jnp.int32), axis=1)


def block_scores(query_part, key_part, query_pos, query_docs, key_pos, key_docs):
    scale = 1.0 / math.sqrt(CHANNEL_DIM)
    logits = (
        jnp.einsum("qagd,kad->agqk", query_part, key_part, preferred_element_type=jnp.float32)
        * scale
    )
    allowed = (key_pos[None, :] <= query_pos[:, None]) & (key_docs[None, :] == query_docs[:, None])
    return (jnp.where(allowed[None, None], logits, masked_score), allowed)


def back_project(grad, weight):
    return lax.dot_general(
        grad, weight, (((1,), (1,)), ((), ())), preferred_element_type=jnp.float32
    )


def stream_stats(
    query_heads,
    grad_heads,
    own_positions,
    own_documents,
    key_blocks,
    value_blocks,
    position_blocks,
    document_blocks,
    kv_heads,
    sharing_bundles,
    tokens,
):

    def gather_stats(carry, item):
        maxima, totals, inner = carry
        key_part, value_part, key_pos, key_docs = item
        logits, allowed = block_scores(
            query_heads, key_part, own_positions, own_documents, key_pos, key_docs
        )
        fresh = jnp.maximum(maxima, jnp.max(logits, axis=3))
        factor = jnp.exp(maxima - fresh)
        weights = jnp.where(allowed[None, None], jnp.exp(logits - fresh[..., None]), 0.0)
        slopes = jnp.einsum(
            "qagd,kad->agqk", grad_heads, value_part, preferred_element_type=jnp.float32
        )
        totals = totals * factor + jnp.sum(weights, axis=3)
        inner = inner * factor + jnp.sum(weights * slopes, axis=3)
        return ((fresh, totals, inner), 0)

    start_max = jnp.full((kv_heads, sharing_bundles, tokens), masked_score, jnp.float32)
    start_sum = jnp.zeros((kv_heads, sharing_bundles, tokens), jnp.float32)
    (maxima, totals, inner), unused = lax.scan(
        gather_stats,
        (start_max, start_sum, start_sum),
        (key_blocks, value_blocks, position_blocks, document_blocks),
    )
    return (maxima, totals, inner / totals)


def shards(inputs, out_grad, w_query, w_key, value_projection, w_out, doc_lengths, span_order):
    tokens = inputs.shape[0]
    half = tokens // 2
    length = span_order.shape[0] * half
    kv_heads = w_key.shape[1] // CHANNEL_DIM
    sharing_bundles = ASKER_NUM // SHARED_KV_NUM
    width = w_key.shape[1]
    scale = 1.0 / math.sqrt(CHANNEL_DIM)
    block = math.gcd(length, 512)
    count = length // block
    offsets = jnp.arange(half, dtype=jnp.int32)
    all_positions = (span_order[:, None] * half + offsets[None, :]).reshape(length)
    all_documents = doc_index(all_positions, doc_lengths)
    mine = lax.axis_index("ctx")
    own_positions = lax.dynamic_slice_in_dim(all_positions, mine * tokens, tokens)
    own_documents = lax.dynamic_slice_in_dim(all_documents, mine * tokens, tokens)
    position_blocks = all_positions.reshape(count, block)
    document_blocks = all_documents.reshape(count, block)
    query = jnp.dot(inputs, w_query, preferred_element_type=jnp.float32).astype(jnp.bfloat16)
    keys = jnp.dot(inputs, w_key, preferred_element_type=jnp.float32).astype(jnp.bfloat16)
    values = jnp.dot(inputs, value_projection, preferred_element_type=jnp.float32).astype(
        jnp.bfloat16
    )
    context_grad = back_project(gathered_copies(out_grad, HEAD, 1), w_out).astype(jnp.bfloat16)
    gathered = lax.all_gather(jnp.concatenate([keys, values], axis=1), "ctx", axis=0, tiled=True)
    paired = gathered.reshape(count, block, 2, kv_heads, CHANNEL_DIM)
    key_blocks = paired[:, :, 0]
    value_blocks = paired[:, :, 1]
    query_heads = query.reshape(tokens, kv_heads, sharing_bundles, CHANNEL_DIM)
    grad_heads = context_grad.reshape(tokens, kv_heads, sharing_bundles, CHANNEL_DIM)
    maxima, totals, delta = stream_stats(
        query_heads,
        grad_heads,
        own_positions,
        own_documents,
        key_blocks,
        value_blocks,
        position_blocks,
        document_blocks,
        kv_heads,
        sharing_bundles,
        tokens,
    )

    def key_side(query_acc, item):
        key_part, value_part, key_pos, key_docs = item
        logits, allowed = block_scores(
            query_heads, key_part, own_positions, own_documents, key_pos, key_docs
        )
        probability = jnp.where(
            allowed[None, None], jnp.exp(logits - maxima[..., None]) / totals[..., None], 0.0
        )
        slopes = jnp.einsum(
            "qagd,kad->agqk", grad_heads, value_part, preferred_element_type=jnp.float32
        )
        score_grad = (probability * (slopes - delta[..., None])).astype(jnp.bfloat16)
        rounded = probability.astype(jnp.bfloat16)
        value_term = jnp.einsum(
            "agqk,qagd->kad", rounded, grad_heads, preferred_element_type=jnp.float32
        )
        key_term = (
            jnp.einsum(
                "agqk,qagd->kad", score_grad, query_heads, preferred_element_type=jnp.float32
            )
            * scale
        )
        query_acc = query_acc + jnp.einsum(
            "agqk,kad->qagd", score_grad, key_part, preferred_element_type=jnp.float32
        )
        return (
            query_acc,
            jnp.concatenate([key_term.reshape(block, -1), value_term.reshape(block, -1)], axis=1),
        )

    query_acc, lookup_pieces = lax.scan(
        key_side,
        jnp.zeros((tokens, kv_heads, sharing_bundles, CHANNEL_DIM), jnp.float32),
        (key_blocks, value_blocks, position_blocks, document_blocks),
    )
    query_grad = (query_acc * scale).reshape(tokens, -1).astype(jnp.bfloat16)
    owned = lax.psum_scatter(
        lookup_pieces.reshape(length, -1), "ctx", scatter_dimension=0, tiled=True
    ).astype(jnp.bfloat16)
    key_gradient = owned[:, :width]
    value_gradient = owned[:, width:]
    partial_value = (
        back_project(query_grad, w_query)
        + back_project(key_gradient, w_key)
        + back_project(value_gradient, value_projection)
    )
    return summed_rows(partial_value, HEAD, (1, 0), 1).astype(jnp.bfloat16)


def solution(mesh):
    split = Mesh(mesh.devices.reshape(2, 4, mesh.shape["ctx"]), ("head_0", "head_1", "ctx"))
    in_specs = (
        P("ctx", None),
        P("ctx", HEAD),
        P(None, HEAD),
        P(None, HEAD),
        P(None, HEAD),
        P(HEAD, None),
        P(),
        P(),
    )
    out_specs = P("ctx", HEAD)
    return jax.shard_map(
        shards, mesh=split, in_specs=in_specs, out_specs=out_specs, check_vma=False
    )
```

profile of v0, /device:TPU:1, one launch (start us, length us, event | category | flops | bytes accessed | tf_op | source)
XLA Modules:
  0.0 305.4 jit_solution(14362531104484745187)
XLA Ops:
  8.1 2.1 convolution_convert_fusion.3
  13.4 8.4 %all-to-all-start = ((bf16[8,256,512]{1,2,0:T(8,128)(2,1)}), bf16[8,256,512]{1,2,0:T(8,128)(2,1)}, u32[]{:S(2)}, u32[]{:S(2)}) async-start(bf16[8,256,512]{1,2,0:T(8,128)(2,1)} %broadcast_in_dim.74), calls=%async_computation | async-start | bytes 4194304 | tf_op jit(solution)/shard_map/all_to_all | solution.py:26
  22.5 3.5 %convolution_convert_fusion.1 = bf16[256,512]{1,0:T(8,128)(2,1)S(1)} fusion(bf16[256,4096]{1,0:T(8,128)(2,1)S(1)} %copy-done, bf16[4096,512]{1,0:T(8,128)(2,1)} %param.14), kind=kOutput, calls=%fused_computation.61 | convolution fusion | flops 1073872896 | bytes 6553600 | tf_op jit(solution)/shard_map/dot_general | solution.py:133
  26.5 30.7 %all-to-all-done = bf16[8,256,512]{1,2,0:T(8,128)(2,1)} async-done(((bf16[8,256,512]{1,2,0:T(8,128)(2,1)}), bf16[8,256,512]{1,2,0:T(8,128)(2,1)}, u32[]{:S(2)}, u32[]{:S(2)}) %all-to-all-start) | async-done | bytes 2097184 | tf_op jit(solution)/shard_map/all_to_all | solution.py:26
  57.2 4.1 %convolution_convert_fusion = bf16[256,512]{1,0:T(8,128)(2,1)S(1)} fusion(bf16[256,4096]{0,1:T(8,128)(2,1)} %bitcast.8, bf16[512,4096]{1,0:T(8,128)(2,1)} %param.17), kind=kOutput, calls=%fused_computation.60 | convolution fusion | flops 1073872896 | bytes 6553600 | tf_op jit(solution)/shard_map/dot_general | solution.py:70
  62.4 2.5 copy.66
  65.0 1.7 copy.65
  67.7 25.7 %while.28 = (s32[]{:T(128)}, f32[1,4,256]{2,1,0:T(4,128)S(1)}, f32[1,4,256]{2,1,0:T(4,128)S(1)}, f32[1,4,256]{2,1,0:T(4,128)S(1)}, s32[8,512]{1,0:T(8,128)S(1)},...) while((s32[]{:T(128)}, f32[1,4,256]{2,1,0:T(4,128)S(1)}, ...), condition=%wide.region_6.7_spmd.clone, body=%wide.region_2.6_spmd.clone.sunk | while | flops 276175872 | bytes 8739008 | solution.py:107
  68.7 1.7 fusion.76
  71.9 1.7 fusion.76
  75.1 1.7 fusion.76
  78.3 1.7 fusion.76
  81.5 1.7 fusion.76
  84.8 1.7 fusion.76
  88.0 1.7 fusion.76
  91.2 1.7 fusion.76
  93.5 37.9 %while.29 = (s32[]{:T(128)}, f32[256,1,4,128]{0,3,2,1:T(8,128)S(1)}, f32[8,512,256]{2,1,0:T(8,128)}, bf16[8,512,1,128]{3,1,2,0:T(8,128)(2,1)S(1)}, s32[8,512]{1,...) while((s32[]{:T(128)}, ...), condition=%wide.region_8.9_spmd.clone, body=%wide.region_7.8_spmd.clone.sunk | while | flops 676659200 | bytes 15886523 | solution.py:189
  131.7 67.9 %reduce-scatter.4.cloned.1.call-done = f32[256,256]{1,0:T(8,128)} async-done(((f32[4096,256]{1,0:T(8,128)}), f32[256,256]{1,0:T(8,128)}) %reduce-scatter.4.cloned.1.call-update) | async-done | bytes 262160 | tf_op jit(solution)/shard_map/reduce_scatter | solution.py:195
  204.8 5.8 %copy.67 = f32[32,8,8,512]{3,2,1,0:T(8,128)} copy(f32[32,8,8,512]{3,1,2,0:T(8,128)S(1)} %bitcast.231) | data formatting | bytes 8388608
  210.6 5.2 %reshape.273 = f32[2,4,256,512]{3,1,0,2:T(4,128)} reshape(f32[8,256,512]{2,0,1:T(8,128)} %bitcast.233) | data formatting | bytes 8388608 | tf_op jit(solution)/shard_map/reshape | solution.py:35
  215.8 6.6 %copy.54 = f32[2,4,256,512]{3,2,0,1:T(8,128)} copy(f32[2,4,256,512]{3,1,0,2:T(4,128)} %reshape.273) | data formatting | bytes 8388608 | tf_op jit(solution)/shard_map/reshape | solution.py:35
  222.5 48.5 %reduce-scatter.6.cloned.1.call-done = f32[2,256,512]{2,1,0:T(8,128)} async-done(((f32[8,256,512]{2,1,0:T(8,128)}), f32[2,256,512]{2,1,0:T(8,128)}) %reduce-scatter.6.cloned.1.call-update) | async-done | bytes 1048592 | tf_op jit(solution)/shard_map/reduce_scatter | solution.py:39
  271.0 26.1 %reduce-scatter.8.cloned.1.call-done = f32[1,256,512]{2,1,0:T(8,128)} async-done(((f32[2,256,512]{2,1,0:T(8,128)}), f32[1,256,512]{2,1,0:T(8,128)}) %reduce-scatter.8.cloned.1.call-update) | async-done | bytes 524304 | tf_op jit(solution)/shard_map/reduce_scatter | solution.py:39
  297.1 1.8 convert_bitcast_fusion
  (213 shorter events, 62.7 us)
Async XLA Ops:
  6.5 1.6 copy-start
  6.5 3.6 %copy-start.3 = (bf16[4096,128]{1,0:T(8,128)(2,1)S(1)}, bf16[4096,128]{1,0:T(8,128)(2,1)}, u32[]{:S(2)}) copy-start(bf16[4096,128]{1,0:T(8,128)(2,1)} %param.16) | copy-start | bytes 3145732
  6.5 55.8 %all-gather.2.cloned.1.call-start = ((), (), s32[]{:S(2)}) async-start(), calls=%async_computation.4 | async-start | bytes 2228224 | tf_op jit(solution)/shard_map/all_gather | solution.py:139
  10.2 1.5 copy-start.6
  13.4 8.5 %copy-start.8 = (s32[8]{0:T(128)S(1)}, s32[8]{0:T(128)}, u32[]{:S(2)}) copy-start(s32[8]{0:T(128)} %param.18) | copy-start | bytes 100
  13.4 8.7 %copy-start.9 = (s32[32]{0:T(128)S(1)}, s32[32]{0:T(128)}, u32[]{:S(2)}) copy-start(s32[32]{0:T(128)} %param.19) | copy-start | bytes 388
  13.4 43.8 %all-to-all-start = ((bf16[8,256,512]{1,2,0:T(8,128)(2,1)}), bf16[8,256,512]{1,2,0:T(8,128)(2,1)}, u32[]{:S(2)}, u32[]{:S(2)}) async-start(bf16[8,256,512]{1,2,0:T(8,128)(2,1)} %broadcast_in_dim.74), calls=%async_computation | async-start | bytes 4194304 | tf_op jit(solution)/shard_map/all_to_all | solution.py:26
  21.8 177.8 %reduce-scatter.4.cloned.1.call-start = ((), (), s32[]{:S(2)}) async-start(), calls=%async_computation.5 | async-start | bytes 4456448 | tf_op jit(solution)/shard_map/reduce_scatter | solution.py:195
  67.7 1.0 copy-start.7
  70.9 1.0 copy-start.7
  74.2 1.0 copy-start.7
  77.4 1.0 copy-start.7
  80.6 1.0 copy-start.7
  83.8 1.0 copy-start.7
  87.0 1.0 copy-start.7
  90.2 1.0 copy-start.7
  131.4 69.1 %copy-start.5 = (bf16[4096,128]{1,0:T(8,128)(2,1)S(1)}, bf16[4096,128]{1,0:T(8,128)(2,1)}, u32[]{:S(2)}) copy-start(bf16[4096,128]{1,0:T(8,128)(2,1)} %param.15) | copy-start | bytes 3145732
  131.4 139.5 %reduce-scatter.6.cloned.1.call-start = ((), (), s32[]{:S(2)}) async-start(), calls=%async_computation.6 | async-start | bytes 5242880 | tf_op jit(solution)/shard_map/reduce_scatter | solution.py:39
  200.5 2.2 copy-start.2
  202.7 1.4 copy-start.4
  222.4 76.4 %copy-start.1 = (bf16[256,4096]{1,0:T(8,128)(2,1)S(1)}, bf16[256,4096]{1,0:T(8,128)(2,1)}, u32[]{:S(2)}) copy-start(bf16[256,4096]{1,0:T(8,128)(2,1)} %param.12) | copy-start | bytes 6291460
  222.4 74.6 %reduce-scatter.8.cloned.1.call-start = ((), (), s32[]{:S(2)}) async-start(), calls=%async_computation.7 | async-start | bytes 1572864 | tf_op jit(solution)/shard_map/reduce_scatter | solution.py:39
Sparse Core Ops, SparseCore 0:
  11.8 45.2 all-gather.1
  131.5 67.9 reduce-scatter.3
  222.5 48.3 reduce-scatter.5
  273.1 23.8 reduce-scatter.7
where the time goes:
time: 306 us; the launch traced here: 305 us
  waiting for transfers between devices  173 us (57%)
  matrix products  57.8 us (19%)
  local copies, waits for them, and re-layouts  39.2 us (13%)
  between operations  13.4 us (4%)
  other arithmetic  11.9 us (4%)
  starting transfers between devices  8.74 us (3%)
    reduce_scatter x2, waiting for transfers between devices, sum_in_order(): parts = lax.psum_scatter(parts, axes[k], scatter_dimension=0, tiled=True)  74.6 us
    reduce_scatter x1, waiting for transfers between devices, shards(): lax.psum_scatter(lookup_pieces.reshape(length, -1), 'ctx', scatter_dimens...  67.9 us
    all_to_all x1, waiting for transfers between devices, copy_for_each(): return lax.all_to_all(copies, axis, split_axis=0, concat_axis=0, tiled=True)  30.7 us
    unnamed x27, local copies, waits for them, and re-layouts  15.3 us
    dot_general x8, matrix products, gather_stats(): jnp.einsum('qagd,kad->agqk', grad_heads, value_part, preferred_element_ty...  13.4 us
    reshape x2, local copies, waits for them, and re-layouts, sum_in_order(): parts = parts.reshape(*lengths, *parts.shape[1:])  11.8 us
    dot_general x8, matrix products, key_side(): jnp.einsum('qagd,kad->agqk', grad_heads, value_part, preferred_element_ty...  10.6 us
    dot_general x16, matrix products, block_scores(): jnp.einsum('qagd,kad->agqk', query_part, key_part, preferred_element_type...  9.65 us
  transfers between devices with their start and end apart: 5, of which 4 were waited for; matrix products, arithmetic and copies ran while one was open for 4% of the time, Pallas kernels for 0%

commit v1 on v0

v1 whole, which is shorter than its diff:
```python
import math

import jax
import jax.numpy as jnp
from jax import lax
from jax.experimental import pallas as pl
from jax.experimental.pallas import tpu as pltpu
from jax.sharding import Mesh
from jax.sharding import PartitionSpec as P

ASKER_NUM = 32
SHARED_KV_NUM = 8
CHANNEL_DIM = 128
HEAD = ("head_0", "head_1")


HALF = 128
TILE = 256
BUNDLE = ASKER_NUM // SHARED_KV_NUM
LOG2E = 1.4426950408889634
MASKED = -1e30


def in_order(parts, dim):
    lengths = list(parts.shape[1:])
    lengths[dim] *= parts.shape[0]
    return jnp.moveaxis(parts, 0, dim).reshape(lengths)


def copy_for_each(value, axis):
    copies = jnp.broadcast_to(value, (lax.axis_size(axis), *value.shape))
    return lax.all_to_all(copies, axis, split_axis=0, concat_axis=0, tiled=True)


def gathered_copies(value, axis, dim):
    return in_order(copy_for_each(value, axis), dim)


def sum_in_order(parts, axes, sequence):
    lengths = [lax.axis_size(a) for a in axes]
    parts = parts.reshape(*lengths, *parts.shape[1:])
    parts = parts.transpose(*sequence, *range(len(axes), parts.ndim))
    parts = parts.reshape(-1, *parts.shape[len(axes) :])
    for k in sequence:
        parts = lax.psum_scatter(parts, axes[k], scatter_dimension=0, tiled=True)
    return parts[0]


def split_up(value, dim, peers):
    lengths = value.shape
    parts = value.reshape(*lengths[:dim], peers, lengths[dim] // peers, *lengths[dim + 1 :])
    return jnp.moveaxis(parts, dim, 0)


def summed_rows(value, axes, sequence, dim):
    peers = lax.axis_size(axes)
    return sum_in_order(split_up(value, dim, peers), axes, sequence)


def back_project(grad, weight):
    return lax.dot_general(
        grad, weight, (((1,), (1,)), ((), ())), preferred_element_type=jnp.float32
    )


def attention_kernel(
    span_ref, block_ref, first_ref, start_ref, q_ref, g_ref, kv_ref,
    dq_ref, dkv_ref,
    kvs, qs, gs, s_buf, d_buf, acc, dqt,
):
    exponent = LOG2E / math.sqrt(CHANNEL_DIM)
    scale = 1.0 / math.sqrt(CHANNEL_DIM)
    spans = span_ref.shape[0]

    @pl.loop(0, spans)
    def _(r):
        p = span_ref[r]
        kvs[pl.ds(pl.multiple_of(p * HALF, HALF), HALF), :] = kv_ref[
            pl.ds(pl.multiple_of(r * HALF, HALF), HALF), :
        ]
        acc[pl.ds(pl.multiple_of(r * HALF, HALF), HALF), :] = jnp.zeros((HALF, 2 * CHANNEL_DIM), jnp.float32)

    lanes = BUNDLE * HALF
    for b in range(2):
        rows = slice(b * HALF, (b + 1) * HALF)
        for h in range(BUNDLE):
            cols = slice(h * CHANNEL_DIM, (h + 1) * CHANNEL_DIM)
            qs[h * HALF : (h + 1) * HALF, :] = q_ref[rows, cols]
            gs[h * HALF : (h + 1) * HALF, :] = g_ref[rows, cols]
        c = block_ref[b]
        low = first_ref[b] // (TILE // HALF)
        high = c // (TILE // HALF) + 1
        start = start_ref[b : b + 1, :]
        position = c * HALF + lax.broadcasted_iota(jnp.int32, (1, HALF), 1)

        def gather_stats(t, carry):
            top, total, inner = carry
            at = pl.ds(pl.multiple_of(t * TILE, TILE), TILE)
            keys = kvs[at, :CHANNEL_DIM]
            values = kvs[at, CHANNEL_DIM:]
            key_position = t * TILE + lax.broadcasted_iota(jnp.int32, (TILE, HALF), 0)
            bias = jnp.where(
                (key_position <= position) & (key_position >= start), 0.0, MASKED
            )
            bias = jnp.concatenate([bias] * BUNDLE, axis=1)
            s = lax.dot_general(
                keys, qs[...], (((1,), (1,)), ((), ())), preferred_element_type=jnp.float32
            )
            s = s * exponent + bias
            s_buf[at, :] = s
            fresh = jnp.maximum(top, jnp.max(s, axis=0, keepdims=True))
            factor = jnp.exp2(top - fresh)
            e = jnp.exp2(s - fresh)
            slopes = lax.dot_general(
                values, gs[...], (((1,), (1,)), ((), ())), preferred_element_type=jnp.float32
            )
            d_buf[at, :] = slopes
            total = total * factor + jnp.sum(e, axis=0, keepdims=True)
            inner = inner * factor + jnp.sum(e * slopes, axis=0, keepdims=True)
            return fresh, total, inner

        zero = jnp.zeros((1, lanes), jnp.float32)
        top, total, inner = lax.fori_loop(
            low, high, gather_stats, (jnp.full((1, lanes), MASKED, jnp.float32), zero, zero)
        )
        delta = inner / total
        level = top + jnp.log2(total)
        dqt[...] = jnp.zeros_like(dqt)

        @pl.loop(low, high)
        def _(t):
            at = pl.ds(pl.multiple_of(t * TILE, TILE), TILE)
            probability = jnp.exp2(s_buf[at, :] - level)
            score_grad = (probability * (d_buf[at, :] - delta)).astype(jnp.bfloat16)
            rounded = probability.astype(jnp.bfloat16)
            acc[at, CHANNEL_DIM:] += jnp.dot(rounded, gs[...], preferred_element_type=jnp.float32)
            acc[at, :CHANNEL_DIM] += jnp.dot(score_grad, qs[...], preferred_element_type=jnp.float32)
            dqt[...] += lax.dot_general(
                kvs[at, :CHANNEL_DIM], score_grad, (((0,), (0,)), ((), ())),
                preferred_element_type=jnp.float32,
            )

        for h in range(BUNDLE):
            dq_ref[rows, h * CHANNEL_DIM : (h + 1) * CHANNEL_DIM] = (
                (dqt[:, h * HALF : (h + 1) * HALF] * scale).T.astype(jnp.bfloat16)
            )

    @pl.loop(0, spans)
    def _(r):
        p = span_ref[r]
        at = pl.ds(pl.multiple_of(p * HALF, HALF), HALF)
        to = pl.ds(pl.multiple_of(r * HALF, HALF), HALF)
        dkv_ref[to, :CHANNEL_DIM] = (acc[at, :CHANNEL_DIM] * scale).astype(jnp.bfloat16)
        dkv_ref[to, CHANNEL_DIM:] = acc[at, CHANNEL_DIM:].astype(jnp.bfloat16)


def attention(q, g, kv, span_order, doc_lengths):
    tokens = q.shape[0]
    length = kv.shape[0]
    ends = jnp.cumsum(doc_lengths)
    mine = lax.axis_index("ctx")
    blocks = lax.dynamic_slice_in_dim(span_order, mine * 2, 2)
    positions = blocks[:, None] * HALF + jnp.arange(HALF, dtype=jnp.int32)[None, :]
    starts = jnp.max(
        jnp.where(positions[:, :, None] >= ends[None, None, :], ends[None, None, :], 0), axis=2
    ).astype(jnp.int32)
    first = (starts[:, 0] // HALF).astype(jnp.int32)
    smem = pl.BlockSpec(memory_space=pltpu.SMEM)
    vmem = pl.BlockSpec(memory_space=pltpu.VMEM)
    lanes = BUNDLE * HALF
    return pl.pallas_call(
        attention_kernel,
        out_shape=(
            jax.ShapeDtypeStruct((tokens, lanes), jnp.bfloat16),
            jax.ShapeDtypeStruct((length, 2 * CHANNEL_DIM), jnp.bfloat16),
        ),
        in_specs=[smem, smem, smem, vmem, vmem, vmem, vmem],
        out_specs=(vmem, vmem),
        scratch_shapes=[
            pltpu.VMEM((length, 2 * CHANNEL_DIM), jnp.bfloat16),
            pltpu.VMEM((lanes, CHANNEL_DIM), jnp.bfloat16),
            pltpu.VMEM((lanes, CHANNEL_DIM), jnp.bfloat16),
            pltpu.VMEM((length, lanes), jnp.float32),
            pltpu.VMEM((length, lanes), jnp.float32),
            pltpu.VMEM((length, 2 * CHANNEL_DIM), jnp.float32),
            pltpu.VMEM((CHANNEL_DIM, lanes), jnp.float32),
        ],
        compiler_params=pltpu.CompilerParams(vmem_limit_bytes=40 * 1024 * 1024),
        name="attention",
    )(span_order, blocks, first, starts, q, g, kv)


def shards(inputs, out_grad, w_query, w_key, value_projection, w_out, doc_lengths, span_order):
    width = w_key.shape[1]
    query = jnp.dot(inputs, w_query, preferred_element_type=jnp.float32).astype(jnp.bfloat16)
    keys = jnp.dot(inputs, w_key, preferred_element_type=jnp.float32).astype(jnp.bfloat16)
    values = jnp.dot(inputs, value_projection, preferred_element_type=jnp.float32).astype(
        jnp.bfloat16
    )
    context_grad = back_project(gathered_copies(out_grad, HEAD, 1), w_out).astype(jnp.bfloat16)
    gathered = lax.all_gather(jnp.concatenate([keys, values], axis=1), "ctx", axis=0, tiled=True)
    query_grad, pieces = attention(query, context_grad, gathered, span_order, doc_lengths)
    owned = lax.psum_scatter(pieces, "ctx", scatter_dimension=0, tiled=True)
    partial_value = (
        back_project(query_grad, w_query)
        + back_project(owned[:, :width], w_key)
        + back_project(owned[:, width:], value_projection)
    )
    return summed_rows(partial_value, HEAD, (1, 0), 1).astype(jnp.bfloat16)


def solution(mesh):
    split = Mesh(mesh.devices.reshape(2, 4, mesh.shape["ctx"]), ("head_0", "head_1", "ctx"))
    in_specs = (
        P("ctx", None),
        P("ctx", HEAD),
        P(None, HEAD),
        P(None, HEAD),
        P(None, HEAD),
        P(HEAD, None),
        P(),
        P(),
    )
    out_specs = P("ctx", HEAD)
    return jax.shard_map(
        shards, mesh=split, in_specs=in_specs, out_specs=out_specs, check_vma=False
    )
```

time: 306 us -> 244 us (0.80)
  matrix products: 57.8 us -> 15.5 us
  local copies, waits for them, and re-layouts: 39.2 us -> 24.2 us
  other arithmetic: 11.9 us -> 2.88 us
  Pallas kernels: 0 us -> 5.33 us
    dot_general x56 -> x0, matrix products: 44.5 us -> none  [the longest x8 13.4 us: gather_stats(): jnp.einsum('qagd,kad->agqk', grad_heads, value_part, preferred_element_ty...]
    dynamic_update_slice x16 -> x0, local copies, waits for them, and re-layouts: 8.25 us -> none  [shards(): lax.scan(key_side, jnp.zeros((tokens, kv_heads, sharing_bundles, CHANNEL_...]
    pallas_call x0 -> x1, Pallas kernels: none -> 5.33 us  [attention(): pl.pallas_call(attention_kernel, out_shape=(jax.ShapeDtypeStruct((tokens,...]
    unnamed x27 -> x20, local copies, waits for them, and re-layouts: 15.3 us -> 10.9 us
    reduce_sum x9 -> x0, other arithmetic: 4.36 us -> none  [the longest x8 4.24 us: gather_stats(): totals = totals * factor + jnp.sum(weights, axis=3)]
    and x16 -> x0, other arithmetic: 3.28 us -> none  [block_scores(): (key_pos[None, :] <= query_pos[:, None]) & (key_docs[None, :] == query_do...]
where the time goes in v1:
time: 244 us; the launch traced here: 242 us
  waiting for transfers between devices  172 us (70%)
  local copies, waits for them, and re-layouts  24.2 us (10%)
  matrix products  15.5 us (6%)
  between operations  13.3 us (5%)
  starting transfers between devices  8.62 us (4%)
  Pallas kernels  5.33 us (2%)
  other arithmetic  2.88 us (1%)
    reduce_scatter x2, waiting for transfers between devices, sum_in_order(): parts = lax.psum_scatter(parts, axes[k], scatter_dimension=0, tiled=True)  75.1 us
    reduce_scatter x1, waiting for transfers between devices, shards(): owned = lax.psum_scatter(pieces, 'ctx', scatter_dimension=0, tiled=True)  65.4 us
    all_to_all x1, waiting for transfers between devices, copy_for_each(): return lax.all_to_all(copies, axis, split_axis=0, concat_axis=0, tiled=True)  31.4 us
    reshape x2, local copies, waits for them, and re-layouts, sum_in_order(): parts = parts.reshape(*lengths, *parts.shape[1:])  11.8 us
    unnamed x20, local copies, waits for them, and re-layouts  10.9 us
    all_to_all x1, starting transfers between devices, copy_for_each(): return lax.all_to_all(copies, axis, split_axis=0, concat_axis=0, tiled=True)  8.31 us
    dot_general x4, matrix products, back_project(): lax.dot_general(grad, weight, (((1,), (1,)), ((), ())), preferred_element...  8.22 us
    pallas_call x1, Pallas kernels, attention(): pl.pallas_call(attention_kernel, out_shape=(jax.ShapeDtypeStruct((tokens,...  5.33 us
  transfers between devices with their start and end apart: 5, of which 4 were waited for; matrix products, arithmetic and copies ran while one was open for 4% of the time, Pallas kernels for 0%

profile of v1, /device:TPU:1, one launch (start us, length us, event | category | flops | bytes accessed | tf_op | source)
XLA Modules:
  0.0 241.7 jit_solution(11080397755136807116)
XLA Ops:
  6.5 1.6 copy-done
  8.1 1.9 convolution_convert_fusion.3
  10.0 1.9 convolution_convert_fusion.2
  12.0 0.7 pad_maximum_fusion
  12.8 1.5 broadcast_in_dim.9
  14.3 8.3 %all-to-all-start = ((bf16[8,256,512]{1,2,0:T(8,128)(2,1)}), bf16[8,256,512]{1,2,0:T(8,128)(2,1)}, u32[]{:S(2)}, u32[]{:S(2)}) async-start(bf16[8,256,512]{1,2,0:T(8,128)(2,1)} %broadcast_in_dim.9), calls=%async_computation | async-start | bytes 4194304 | tf_op jit(solution)/shard_map/all_to_all | solution.py:32
  23.2 3.4 %convolution_convert_fusion.1.q_ref = bf16[256,512]{1,0:T(8,128)(2,1)S(1)} fusion(bf16[256,4096]{1,0:T(8,128)(2,1)S(1)} %copy-done, bf16[4096,512]{1,0:T(8,128)(2,1)} %param.10), kind=kOutput, calls=%fused_computation.3 | convolution fusion | flops 1073872896 | bytes 6553600 | tf_op jit(solution)/shard_map/dot_general | solution.py:195
  26.7 31.4 %all-to-all-done = bf16[8,256,512]{1,2,0:T(8,128)(2,1)} async-done(((bf16[8,256,512]{1,2,0:T(8,128)(2,1)}), bf16[8,256,512]{1,2,0:T(8,128)(2,1)}, u32[]{:S(2)}, u32[]{:S(2)}) %all-to-all-start) | async-done | bytes 2097184 | tf_op jit(solution)/shard_map/all_to_all | solution.py:32
  58.0 4.1 %convolution_convert_fusion.g_ref = bf16[256,512]{1,0:T(8,128)(2,1)S(1)} fusion(bf16[256,4096]{0,1:T(8,128)(2,1)} %bitcast.3, bf16[512,4096]{1,0:T(8,128)(2,1)} %param.13), kind=kOutput, calls=%fused_computation.2 | convolution fusion | flops 1073872896 | bytes 6553600 | tf_op jit(solution)/shard_map/dot_general | solution.py:61
  62.2 1.6 copy-done.1
  63.8 5.3 %attention.1 = (bf16[256,512]{1,0:T(8,128)(2,1)S(1)}, bf16[4096,256]{1,0:T(8,128)(2,1)S(1)}) custom-call(s32[32]{0:T(128)S(1)} %copy-done.3, s32[2]{0:T(128)S(1)} %get-tuple-element.10.block_ref, s32[2]{0:T(128)S(1)} %and_select_fusion.first_ref, s32[2,128]{1,0:T(2,128)S(1)} %select_reduce_fusion.start_ref, ...), custom_call_target="tpu_custom_call" | custom-call | tf_op jit(solution)/shard_map/attention/pallas_call | solution.py:171
  69.1 1.3 copy-done.2
  70.5 0.2 reduce-scatter.6.cloned.1.call-start
  70.7 65.4 %reduce-scatter.4.cloned.1.call-done = bf16[256,256]{1,0:T(8,128)(2,1)} async-done(((bf16[4096,256]{1,0:T(8,128)(2,1)}), bf16[256,256]{1,0:T(8,128)(2,1)}) %reduce-scatter.4.cloned.1.call-update) | async-done | bytes 131088 | tf_op jit(solution)/shard_map/reduce_scatter | solution.py:203
  136.1 2.1 fusion.1
  138.2 0.4 copy-done.4
  138.6 1.3 convolution_add_fusion
  140.0 0.7 convolution_add_fusion.1
  140.7 5.8 %copy.22 = f32[32,8,8,512]{3,2,1,0:T(8,128)} copy(f32[32,8,8,512]{3,1,2,0:T(8,128)S(1)} %bitcast.28) | data formatting | bytes 8388608
  146.4 5.2 %reshape.63 = f32[2,4,256,512]{3,1,0,2:T(4,128)} reshape(f32[8,256,512]{2,0,1:T(8,128)} %bitcast.30) | data formatting | bytes 8388608 | tf_op jit(solution)/shard_map/reshape | solution.py:41
  151.6 6.6 %copy.19 = f32[2,4,256,512]{3,2,0,1:T(8,128)} copy(f32[2,4,256,512]{3,1,0,2:T(4,128)} %reshape.63) | data formatting | bytes 8388608 | tf_op jit(solution)/shard_map/reshape | solution.py:41
  158.3 49.0 %reduce-scatter.6.cloned.1.call-done = f32[2,256,512]{2,1,0:T(8,128)} async-done(((f32[8,256,512]{2,1,0:T(8,128)}), f32[2,256,512]{2,1,0:T(8,128)}) %reduce-scatter.6.cloned.1.call-update) | async-done | bytes 1048592 | tf_op jit(solution)/shard_map/reduce_scatter | solution.py:45
  207.3 26.1 %reduce-scatter.8.cloned.1.call-done = f32[1,256,512]{2,1,0:T(8,128)} async-done(((f32[2,256,512]{2,1,0:T(8,128)}), f32[1,256,512]{2,1,0:T(8,128)}) %reduce-scatter.8.cloned.1.call-update) | async-done | bytes 524304 | tf_op jit(solution)/shard_map/reduce_scatter | solution.py:45
  233.4 1.8 convert_bitcast_fusion
  (29 shorter events, 0.9 us)
Async XLA Ops:
  6.5 1.6 copy-start
  6.5 6.2 %copy-start.6 = (bf16[256,512]{1,0:T(8,128)(2,1)S(1)}, bf16[256,512]{1,0:T(8,128)(2,1)}, u32[]{:S(2)}) copy-start(bf16[256,512]{1,0:T(8,128)(2,1)} %param.9) | copy-start | bytes 786436
  6.5 55.6 %all-gather.2.cloned.1.call-start = ((), (), s32[]{:S(2)}) async-start(), calls=%async_computation.4 | async-start | bytes 2228224 | tf_op jit(solution)/shard_map/all_gather | solution.py:201
  12.0 10.7 %copy-start.8 = (s32[8]{0:T(128)S(1)}, s32[8]{0:T(128)}, u32[]{:S(2)}) copy-start(s32[8]{0:T(128)} %param.14) | copy-start | bytes 100
  12.0 10.9 %copy-start.3 = (s32[32]{0:T(128)S(1)}, s32[32]{0:T(128)}, u32[]{:S(2)}) copy-start(s32[32]{0:T(128)} %span_ref.1) | copy-start | bytes 388
  14.3 43.7 %all-to-all-start = ((bf16[8,256,512]{1,2,0:T(8,128)(2,1)}), bf16[8,256,512]{1,2,0:T(8,128)(2,1)}, u32[]{:S(2)}, u32[]{:S(2)}) async-start(bf16[8,256,512]{1,2,0:T(8,128)(2,1)} %broadcast_in_dim.9), calls=%async_computation | async-start | bytes 4194304 | tf_op jit(solution)/shard_map/all_to_all | solution.py:32
  22.6 113.5 %reduce-scatter.4.cloned.1.call-start = ((), (), s32[]{:S(2)}) async-start(), calls=%async_computation.5 | async-start | bytes 2228224 | tf_op jit(solution)/shard_map/reduce_scatter | solution.py:203
  62.2 1.6 copy-start.1
  69.1 1.3 copy-start.2
  70.5 136.8 %reduce-scatter.6.cloned.1.call-start = ((), (), s32[]{:S(2)}) async-start(), calls=%async_computation.6 | async-start | bytes 5242880 | tf_op jit(solution)/shard_map/reduce_scatter | solution.py:45
  136.1 2.5 %copy-start.4 = (bf16[4096,512]{1,0:T(8,128)(2,1)S(1)}, bf16[4096,512]{1,0:T(8,128)(2,1)}, u32[]{:S(2)}) copy-start(bf16[4096,512]{1,0:T(8,128)(2,1)} %param.10) | copy-start | bytes 12582916
  138.6 1.3 copy-start.5
  138.6 1.3 copy-start.7
  158.2 75.1 %reduce-scatter.8.cloned.1.call-start = ((), (), s32[]{:S(2)}) async-start(), calls=%async_computation.7 | async-start | bytes 1572864 | tf_op jit(solution)/shard_map/reduce_scatter | solution.py:45
Sparse Core Ops, SparseCore 0:
  12.8 39.7 all-gather.1
  70.6 65.4 reduce-scatter.3
  158.4 48.8 reduce-scatter.5
  209.5 23.8 reduce-scatter.7
